TPU v7x, 512 devices: a whole 4x8x8 slice. The times are simulated.
512 devices in a mesh: bin: 64 (over z, x, y_hi), grp: 8 (over y_lo, core).
Axes of the slice: x: 4, y: 8 (y_hi: 2, y_lo: 4; y = y_hi * 4 + y_lo), z: 8, core: 2. Of those that a mesh axis runs over, the one named last changes fastest.
Arguments:
- record: bfloat16 [8, 256, 8704], P('grp', 'bin'), may hold values from -60 to 60
- ref_index: int32 [8, 16], P('grp'), may hold values from 0 to 255, as said below
- offsets: int32 [16], replicated, may hold values from 0 to 7680, as said below
Outputs:
- transfer: bfloat16 [512, 2048, 256], P('bin', 'grp')
Inputs may be any that keep to these rules, and one draw needn't show every extreme that they name: `ref_index`: each row lists 16 different channels of its group; every row holds 0 and 255. `offsets`: starts rise; the first is 0, the last is 7680, and neighbours lie 512 // 2 to 768 apart.
All inputs are finite; a program needn't handle non-finite values.
Results may differ from a plain program's by a relative error of at most 0.0095.
Values may be sent and summed in bfloat16 or wider, within the bound.
A program may use at most 64 MiB of HBM per device.

v0:
```python
import math
import jax
import jax.numpy as jnp
from jax import lax
from jax.sharding import PartitionSpec as P

L = 1024
NB = 512
ridge_weight = 0.5


def make_table(seg_len, bins):
    sample_num = lax.iota(jnp.int32, seg_len)[:, None]
    bin_num = lax.iota(jnp.int32, bins)[None, :]
    angles = (sample_num * bin_num % seg_len).astype(jnp.float32) * (2.0 * math.pi / seg_len)
    hann_window = 0.5 - 0.5 * jnp.cos(sample_num.astype(jnp.float32) * (2.0 * math.pi / seg_len))
    return jnp.concatenate(
        [hann_window * jnp.cos(angles), -(hann_window * jnp.sin(angles))], axis=1
    ).astype(jnp.bfloat16)


def transform(chan_rows, starts, dft_table, bin_devices):
    seg_len = dft_table.shape[0]
    pieces = jax.vmap(lambda start_at: lax.dynamic_slice_in_dim(chan_rows, start_at, seg_len, 1))(
        starts
    )
    spectra = jnp.einsum(
        "scn,nk->ksc", pieces, dft_table, preferred_element_type=jnp.float32
    ).astype(jnp.bfloat16)
    bin_total = dft_table.shape[1] // 2
    return spectra.reshape(
        2, bin_devices, bin_total // bin_devices, starts.shape[0], chan_rows.shape[0]
    )


def local(record, ref_index, offsets):
    chan_rows = record[0]
    dft_table = make_table(L, NB)
    bin_devices = lax.axis_size("bin")
    spectra = transform(chan_rows, offsets, dft_table, bin_devices)
    channels = lax.all_to_all(spectra, "bin", split_axis=1, concat_axis=4, tiled=True)[:, 0]
    local_refs = jnp.take(channels, ref_index[0], axis=3)
    references = lax.all_gather(local_refs, "grp", axis=3, tiled=True)
    ref_real = references[0]
    ref_imag = references[1]
    ref_blocks = jnp.stack(
        [
            jnp.concatenate([ref_real, -ref_imag], axis=-1),
            jnp.concatenate([ref_imag, ref_real], axis=-1),
        ]
    )
    bins_here = channels.shape[1]
    group_size = math.gcd(bins_here, 4)
    group_count = bins_here // group_size
    real_order = ref_blocks.shape[-1]

    def solve_group(group_index):
        first_bin = group_index * group_size
        ref_group = lax.dynamic_slice_in_dim(ref_blocks, first_bin, group_size, 1)
        chan_group = lax.dynamic_slice_in_dim(channels, first_bin, group_size, 1)
        cross_part = jnp.einsum(
            "pfsr,pfsc->frc", ref_group, chan_group, preferred_element_type=jnp.float32
        )
        auto_part = jnp.einsum(
            "pfsr,pfsq->frq", ref_group, ref_group, preferred_element_type=jnp.float32
        )
        ridge_term = ridge_weight * jnp.trace(auto_part, axis1=1, axis2=2) / real_order
        factor = jnp.linalg.cholesky(
            auto_part + ridge_term[:, None, None] * jnp.eye(real_order, dtype=jnp.float32)
        )
        transfer_t = jax.scipy.linalg.cho_solve((factor, True), cross_part)
        return jnp.swapaxes(transfer_t, 1, 2).astype(jnp.bfloat16)

    results = lax.map(solve_group, jnp.arange(group_count))
    return results.reshape(bins_here, results.shape[2], results.shape[3])


def solution(mesh):
    placed = (P("grp", "bin", None), P("grp", None), P())
    return jax.shard_map(
        local, mesh=mesh, in_specs=placed, out_specs=P("bin", "grp", None), check_vma=False
    )
```

profile of v0, /device:TPU:1, one launch (start us, length us, event | category | flops | bytes accessed | tf_op | source)
XLA Modules:
  0.0 550.2 jit_solution(7552281096765540275)
XLA Ops:
  0.1 8.9 %multiply_convert_fusion = (bf16[1024,512]{1,0:T(8,128)(2,1)S(1)}, bf16[1024,512]{1,0:T(8,128)(2,1)S(1)}) fusion(f32[1024]{0:T(1024)S(1)} %multiply_subtract_fusion), kind=kLoop, calls=%fused_computation.58 | loop fusion | flops 9961472 | bytes 2101248 | tf_op jit(solution)/shard_map/convert.2
  9.0 32.3 %while.17 = (s32[]{:T(128)}, bf16[4,8704]{1,0:T(4,128)(2,1)}, s32[16,2]{0,1:T(2,128)S(1)}, bf16[16,4,1024]{2,1,0:T(4,128)(2,1)S(1)}, s32[]{:T(128)}) while((s32[]{:T(128)}, bf16[4,8704]{1,0:T(4,128)(2,1)}, s32[16,2]{0,1:T(2,128)S(1)}, bf16[16,4,1024]{2,1,0:T(4,128)(2,1)S(1)}, s32[]{:T(128)}) %tuple.87), condition=%wide.while_cond.1, body=%wide.while_body.1.sunk | while | flops 2 | bytes 16481 | solution.py:24
  9.6 1.4 bitcast_dynamic-update-slice_fusion.4
  11.6 1.4 bitcast_dynamic-update-slice_fusion.4
  13.6 1.4 bitcast_dynamic-update-slice_fusion.4
  15.7 1.4 bitcast_dynamic-update-slice_fusion.4
  17.7 1.4 bitcast_dynamic-update-slice_fusion.4
  19.7 1.4 bitcast_dynamic-update-slice_fusion.4
  21.7 1.4 bitcast_dynamic-update-slice_fusion.4
  23.7 1.4 bitcast_dynamic-update-slice_fusion.4
  25.7 1.4 bitcast_dynamic-update-slice_fusion.4
  27.7 1.4 bitcast_dynamic-update-slice_fusion.4
  29.8 1.4 bitcast_dynamic-update-slice_fusion.4
  31.8 1.4 bitcast_dynamic-update-slice_fusion.4
  33.8 1.4 bitcast_dynamic-update-slice_fusion.4
  35.8 1.4 bitcast_dynamic-update-slice_fusion.4
  37.8 1.4 bitcast_dynamic-update-slice_fusion.4
  39.8 1.4 bitcast_dynamic-update-slice_fusion.4
  42.5 1.8 reshape.166
  44.3 19.6 %all-to-all-start = ((bf16[64,2,512]{2,1,0:T(2,128)(2,1)}), bf16[64,2,512]{2,1,0:T(2,128)(2,1)S(1)}, u32[]{:S(2)}, u32[]{:S(2)}) async-start(bf16[64,2,512]{2,1,0:T(2,128)(2,1)} %reshape.166), calls=%async_computation | async-start | bytes 262144 | tf_op jit(solution)/shard_map/all_to_all | solution.py:41
  63.9 13.6 %all-to-all-done = bf16[64,2,512]{2,1,0:T(2,128)(2,1)S(1)} async-done(((bf16[64,2,512]{2,1,0:T(2,128)(2,1)}), bf16[64,2,512]{2,1,0:T(2,128)(2,1)S(1)}, u32[]{:S(2)}, u32[]{:S(2)}) %all-to-all-start) | async-done | bytes 131104 | tf_op jit(solution)/shard_map/all_to_all | solution.py:41
  77.5 0.7 reshape.167
  79.2 16.7 %all_gather.3 = bf16[2,8,16,128]{2,1,0,3:T(8,128)(2,1)S(1)} all-gather(bf16[2,8,16,16]{2,1,0,3:T(8,128)(2,1)S(1)} %select_bitcast_fusion.1), channel_id=1, replica_groups=mesh['bin'=64,'grp'=8] {'grp'}, dimensions={3}, use_global_device_ids=true | all-gather | bytes 73728 | tf_op jit(solution)/shard_map/all_gather | solution.py:43
  96.6 0.8 copy.60
  97.5 452.7 %while.16 = (s32[]{:T(128)}, bf16[2,4,256,256]{3,2,1,0:T(8,128)(2,1)}, s32[2]{0:T(128)S(1)}, bf16[2,8,16,256]{3,2,1,0:T(8,128)(2,1)S(1)}, bf16[2,8,16,256]{3,2,0...) while((s32[]{:T(128)}, ...), condition=%wide.region_6.7_spmd, body=%wide.region_0.6_spmd.sunk | while | flops 1448117248 | bytes 37234176 | solution.py:74
  100.1 46.9 %custom-call.42 = f32[4,128,128]{2,1,0:T(8,128)S(1)} custom-call(f32[4,128,128]{2,1,0:T(8,128)S(1)} %cholesky.172), custom_call_target="Cholesky" | custom-call | tf_op jit(solution)/shard_map/while/body/eval_jaxpr/jit(cholesky)/cholesky | solution.py:68
  147.1 39.3 %custom-call.43 = f32[4,1,128,128]{2,3,1,0:T(8,128)S(1)} custom-call(f32[4,1,128,128]{3,2,1,0:T(8,128)S(1)} %select_bitcast_fusion.3), custom_call_target="InvertDiagBlocksLowerTriangular" | custom-call | tf_op jit(solution)/shard_map/while/body/eval_jaxpr/jit(cholesky)/cholesky | solution.py:68
  186.9 0.7 convolution_subtract_fusion.6
  187.5 46.9 %custom-call.44 = f32[4,128,128]{2,1,0:T(8,128)S(1)} custom-call(f32[4,128,128]{2,1,0:T(8,128)S(1)} %convolution_subtract_fusion.6), custom_call_target="Cholesky" | custom-call | tf_op jit(solution)/shard_map/while/body/eval_jaxpr/jit(cholesky)/cholesky | solution.py:68
  235.1 3.9 while.18
  235.7 1.3 bitcast_dynamic-update-slice_fusion.5
  237.7 1.3 bitcast_dynamic-update-slice_fusion.5
  239.0 78.6 %custom-call.46 = f32[4,2,128,128]{2,3,1,0:T(8,128)S(1)} custom-call(f32[4,2,128,128]{3,2,1,0:T(8,128)S(1)} %bitcast.144), custom_call_target="InvertDiagBlocksLowerTriangular" | custom-call | tf_op jit(solution)/shard_map/while/body/eval_jaxpr/jit(_cho_solve)/vmap()/triangular_solve | solution.py:71
  318.0 0.6 fusion.71
  320.4 0.6 convolution_subtract_fusion.8
  321.9 1.0 copy-done
  323.0 1.0 copy-done.1
  326.3 46.9 %custom-call.42 = f32[4,128,128]{2,1,0:T(8,128)S(1)} custom-call(f32[4,128,128]{2,1,0:T(8,128)S(1)} %cholesky.172), custom_call_target="Cholesky" | custom-call | tf_op jit(solution)/shard_map/while/body/eval_jaxpr/jit(cholesky)/cholesky | solution.py:68
  373.4 39.3 %custom-call.43 = f32[4,1,128,128]{2,3,1,0:T(8,128)S(1)} custom-call(f32[4,1,128,128]{3,2,1,0:T(8,128)S(1)} %select_bitcast_fusion.3), custom_call_target="InvertDiagBlocksLowerTriangular" | custom-call | tf_op jit(solution)/shard_map/while/body/eval_jaxpr/jit(cholesky)/cholesky | solution.py:68
  413.1 0.7 convolution_subtract_fusion.6
  413.8 46.9 %custom-call.44 = f32[4,128,128]{2,1,0:T(8,128)S(1)} custom-call(f32[4,128,128]{2,1,0:T(8,128)S(1)} %convolution_subtract_fusion.6), custom_call_target="Cholesky" | custom-call | tf_op jit(solution)/shard_map/while/body/eval_jaxpr/jit(cholesky)/cholesky | solution.py:68
  461.3 3.9 while.18
  462.0 1.3 bitcast_dynamic-update-slice_fusion.5
  463.9 1.3 bitcast_dynamic-update-slice_fusion.5
  465.3 78.6 %custom-call.46 = f32[4,2,128,128]{2,3,1,0:T(8,128)S(1)} custom-call(f32[4,2,128,128]{3,2,1,0:T(8,128)S(1)} %bitcast.144), custom_call_target="InvertDiagBlocksLowerTriangular" | custom-call | tf_op jit(solution)/shard_map/while/body/eval_jaxpr/jit(_cho_solve)/vmap()/triangular_solve | solution.py:71
  546.7 0.6 convolution_subtract_fusion.8
  548.2 1.0 copy-done
  549.2 1.0 copy-done.1
  (132 shorter events, 27.9 us)
Async XLA Ops:
  0.1 8.9 %copy-start.2 = (s32[16]{0:T(128)S(1)}, s32[16]{0:T(128)}, u32[]{:S(2)}) copy-start(s32[16]{0:T(128)} %param.7) | copy-start | bytes 196
  42.5 21.4 %copy-start.3 = (s32[1,16]{1,0:T(1,128)S(1)}, s32[1,16]{1,0:T(1,128)}, u32[]{:S(2)}) copy-start(s32[1,16]{1,0:T(1,128)} %param.6) | copy-start | bytes 196
  44.3 33.2 %all-to-all-start = ((bf16[64,2,512]{2,1,0:T(2,128)(2,1)}), bf16[64,2,512]{2,1,0:T(2,128)(2,1)S(1)}, u32[]{:S(2)}, u32[]{:S(2)}) async-start(bf16[64,2,512]{2,1,0:T(2,128)(2,1)} %reshape.166), calls=%async_computation | async-start | bytes 262144 | tf_op jit(solution)/shard_map/all_to_all | solution.py:41
  321.7 1.2 copy-start
  322.9 1.0 copy-start.1
  547.9 1.2 copy-start
  549.2 1.0 copy-start.1
where the time goes:
time: 552 us; the launch traced here: 550 us
  other arithmetic  435 us (79%)
  local copies, waits for them, and re-layouts  52.2 us (9%)
  starting transfers between devices  19.6 us (4%)
  blocking collectives  16.7 us (3%)
  waiting for transfers between devices  13.6 us (2%)
  matrix products  11.5 us (2%)
    another operation x20, other arithmetic, solve_group(): jnp.linalg.cholesky(auto_part + ridge_term[:, None, None] * jnp.eye(real_...  267 us
    another operation x8, other arithmetic, solve_group(): transfer_t = jax.scipy.linalg.cho_solve((factor, True), cross_part)  158 us
    gather x48, local copies, waits for them, and re-layouts  32.2 us
    all_to_all x1, starting transfers between devices, local(): lax.all_to_all(spectra, 'bin', split_axis=1, concat_axis=4, tiled=True)  19.6 us
    all_gather x1, blocking collectives, local(): references = lax.all_gather(local_refs, 'grp', axis=3, tiled=True)  16.7 us
    all_to_all x1, waiting for transfers between devices, local(): lax.all_to_all(spectra, 'bin', split_axis=1, concat_axis=4, tiled=True)  13.6 us
  transfers between devices with their start and end apart: 1, of which 1 were waited for; matrix products, arithmetic and copies ran while one was open for 0% of the time, Pallas kernels for 0%

commit v1 on v0

--- a/solution.py
+++ b/solution.py
@@ -1,12 +1,27 @@
+import functools
 import math
 import jax
 import jax.numpy as jnp
 from jax import lax
 from jax.sharding import PartitionSpec as P
+from jax.lax import all_to_all, axis_size
 
 L = 1024
 NB = 512
 ridge_weight = 0.5
+
+
+def match_the_record(mat, named_axis, array_axis, d0):
+    new = jnp.concatenate(
+        all_to_all(
+            jnp.stack(jnp.split(mat, axis_size(named_axis), axis=array_axis)), named_axis, 0, 0
+        ),
+        d0,
+    )
+    return new
+
+
+answer_task = functools.partial(match_the_record, named_axis="bin", array_axis=1, d0=4)
 
 
 def make_table(seg_len, bins):
@@ -38,7 +53,7 @@
     dft_table = make_table(L, NB)
     bin_devices = lax.axis_size("bin")
     spectra = transform(chan_rows, offsets, dft_table, bin_devices)
-    channels = lax.all_to_all(spectra, "bin", split_axis=1, concat_axis=4, tiled=True)[:, 0]
+    channels = answer_task(spectra)[:, 0]
     local_refs = jnp.take(channels, ref_index[0], axis=3)
     references = lax.all_gather(local_refs, "grp", axis=3, tiled=True)
     ref_real = references[0]

time: 552 us -> 553 us (level)
  no operation moved by 1% of the time
where the time goes in v1:
time: 553 us; the launch traced here: 552 us
  other arithmetic  435 us (79%)
  local copies, waits for them, and re-layouts  53.4 us (10%)
  starting transfers between devices  19.6 us (4%)
  blocking collectives  16.7 us (3%)
  waiting for transfers between devices  13.6 us (2%)
  matrix products  11.5 us (2%)
    another operation x20, other arithmetic, solve_group(): jnp.linalg.cholesky(auto_part + ridge_term[:, None, None] * jnp.eye(real_...  267 us
    another operation x8, other arithmetic, solve_group(): transfer_t = jax.scipy.linalg.cho_solve((factor, True), cross_part)  158 us
    gather x48, local copies, waits for them, and re-layouts  32.2 us
    all_to_all x1, starting transfers between devices, match_the_record(): all_to_all(jnp.stack(jnp.split(mat, axis_size(named_axis), axis=array_axi...  19.6 us
    all_gather x1, blocking collectives, local(): references = lax.all_gather(local_refs, 'grp', axis=3, tiled=True)  16.7 us
    all_to_all x1, waiting for transfers between devices, match_the_record(): all_to_all(jnp.stack(jnp.split(mat, axis_size(named_axis), axis=array_axi...  13.6 us
  transfers between devices with their start and end apart: 1, of which 1 were waited for; matrix products, arithmetic and copies ran while one was open for 0% of the time, Pallas kernels for 0%

profile of v1, /device:TPU:1, one launch (start us, length us, event | category | flops | bytes accessed | tf_op | source)
XLA Modules:
  0.0 551.7 jit_solution(8271797535921330326)
XLA Ops:
  0.1 8.9 %multiply_convert_fusion = (bf16[1024,512]{1,0:T(8,128)(2,1)S(1)}, bf16[1024,512]{1,0:T(8,128)(2,1)S(1)}) fusion(f32[1024]{0:T(1024)S(1)} %multiply_subtract_fusion), kind=kLoop, calls=%fused_computation.58 | loop fusion | flops 9961472 | bytes 2101248 | tf_op jit(solution)/shard_map/convert.2
  9.0 32.3 %while.17 = (s32[]{:T(128)}, bf16[4,8704]{1,0:T(4,128)(2,1)}, s32[16,2]{0,1:T(2,128)S(1)}, bf16[16,4,1024]{2,1,0:T(4,128)(2,1)S(1)}, s32[]{:T(128)}) while((s32[]{:T(128)}, bf16[4,8704]{1,0:T(4,128)(2,1)}, s32[16,2]{0,1:T(2,128)S(1)}, bf16[16,4,1024]{2,1,0:T(4,128)(2,1)S(1)}, s32[]{:T(128)}) %tuple.88), condition=%wide.while_cond.1, body=%wide.while_body.1.sunk | while | flops 2 | bytes 16481 | solution.py:39
  9.6 1.4 bitcast_dynamic-update-slice_fusion.4
  11.6 1.4 bitcast_dynamic-update-slice_fusion.4
  13.6 1.4 bitcast_dynamic-update-slice_fusion.4
  15.7 1.4 bitcast_dynamic-update-slice_fusion.4
  17.7 1.4 bitcast_dynamic-update-slice_fusion.4
  19.7 1.4 bitcast_dynamic-update-slice_fusion.4
  21.7 1.4 bitcast_dynamic-update-slice_fusion.4
  23.7 1.4 bitcast_dynamic-update-slice_fusion.4
  25.7 1.4 bitcast_dynamic-update-slice_fusion.4
  27.7 1.4 bitcast_dynamic-update-slice_fusion.4
  29.8 1.4 bitcast_dynamic-update-slice_fusion.4
  31.8 1.4 bitcast_dynamic-update-slice_fusion.4
  33.8 1.4 bitcast_dynamic-update-slice_fusion.4
  35.8 1.4 bitcast_dynamic-update-slice_fusion.4
  37.8 1.4 bitcast_dynamic-update-slice_fusion.4
  39.8 1.4 bitcast_dynamic-update-slice_fusion.4
  43.8 1.8 reshape.169
  45.6 19.6 %all-to-all-start = ((bf16[64,2,512]{2,1,0:T(2,128)(2,1)}), bf16[64,2,512]{2,1,0:T(2,128)(2,1)S(1)}, u32[]{:S(2)}, u32[]{:S(2)}) async-start(bf16[64,2,512]{2,1,0:T(2,128)(2,1)} %reshape.169), calls=%async_computation | async-start | bytes 262144 | tf_op jit(solution)/shard_map/all_to_all | solution.py:16
  65.3 13.6 %all-to-all-done = bf16[64,2,512]{2,1,0:T(2,128)(2,1)S(1)} async-done(((bf16[64,2,512]{2,1,0:T(2,128)(2,1)}), bf16[64,2,512]{2,1,0:T(2,128)(2,1)S(1)}, u32[]{:S(2)}, u32[]{:S(2)}) %all-to-all-start) | async-done | bytes 131104 | tf_op jit(solution)/shard_map/all_to_all | solution.py:16
  78.8 0.7 reshape.170
  80.9 16.7 %all_gather.3 = bf16[2,8,16,128]{2,1,0,3:T(8,128)(2,1)S(1)} all-gather(bf16[2,8,16,16]{2,1,0,3:T(8,128)(2,1)S(1)} %select_bitcast_fusion.1), channel_id=1, replica_groups=mesh['bin'=64,'grp'=8] {'grp'}, dimensions={3}, use_global_device_ids=true | all-gather | bytes 73728 | tf_op jit(solution)/shard_map/all_gather | solution.py:58
  97.6 0.7 copy.398
  99.0 452.7 %while.16 = (s32[]{:T(128)}, bf16[2,4,256,256]{3,2,1,0:T(8,128)(2,1)}, s32[2]{0:T(128)S(1)}, bf16[2,8,16,256]{3,2,1,0:T(8,128)(2,1)S(1)}, bf16[2,8,16,256]{3,2,0...) while((s32[]{:T(128)}, ...), condition=%wide.region_6.7_spmd, body=%wide.region_0.6_spmd.sunk | while | flops 1448117248 | bytes 37234176 | solution.py:89
  101.6 46.9 %custom-call.44 = f32[4,128,128]{2,1,0:T(8,128)S(1)} custom-call(f32[4,128,128]{2,1,0:T(8,128)S(1)} %cholesky.172), custom_call_target="Cholesky" | custom-call | tf_op jit(solution)/shard_map/while/body/eval_jaxpr/jit(cholesky)/cholesky | solution.py:83
  148.6 39.3 %custom-call.45 = f32[4,1,128,128]{2,3,1,0:T(8,128)S(1)} custom-call(f32[4,1,128,128]{3,2,1,0:T(8,128)S(1)} %select_bitcast_fusion.3), custom_call_target="InvertDiagBlocksLowerTriangular" | custom-call | tf_op jit(solution)/shard_map/while/body/eval_jaxpr/jit(cholesky)/cholesky | solution.py:83
  188.4 0.7 convolution_subtract_fusion.6
  189.0 46.9 %custom-call.46 = f32[4,128,128]{2,1,0:T(8,128)S(1)} custom-call(f32[4,128,128]{2,1,0:T(8,128)S(1)} %convolution_subtract_fusion.6), custom_call_target="Cholesky" | custom-call | tf_op jit(solution)/shard_map/while/body/eval_jaxpr/jit(cholesky)/cholesky | solution.py:83
  236.6 3.9 while.18
  237.2 1.3 bitcast_dynamic-update-slice_fusion.5
  239.2 1.3 bitcast_dynamic-update-slice_fusion.5
  240.5 78.6 %custom-call.48 = f32[4,2,128,128]{2,3,1,0:T(8,128)S(1)} custom-call(f32[4,2,128,128]{3,2,1,0:T(8,128)S(1)} %bitcast.583), custom_call_target="InvertDiagBlocksLowerTriangular" | custom-call | tf_op jit(solution)/shard_map/while/body/eval_jaxpr/jit(_cho_solve)/vmap()/triangular_solve | solution.py:86
  321.9 0.6 convolution_subtract_fusion.8
  323.4 1.0 copy-done
  324.5 1.0 copy-done.1
  327.8 46.9 %custom-call.44 = f32[4,128,128]{2,1,0:T(8,128)S(1)} custom-call(f32[4,128,128]{2,1,0:T(8,128)S(1)} %cholesky.172), custom_call_target="Cholesky" | custom-call | tf_op jit(solution)/shard_map/while/body/eval_jaxpr/jit(cholesky)/cholesky | solution.py:83
  374.9 39.3 %custom-call.45 = f32[4,1,128,128]{2,3,1,0:T(8,128)S(1)} custom-call(f32[4,1,128,128]{3,2,1,0:T(8,128)S(1)} %select_bitcast_fusion.3), custom_call_target="InvertDiagBlocksLowerTriangular" | custom-call | tf_op jit(solution)/shard_map/while/body/eval_jaxpr/jit(cholesky)/cholesky | solution.py:83
  414.6 0.7 convolution_subtract_fusion.6
  415.3 46.9 %custom-call.46 = f32[4,128,128]{2,1,0:T(8,128)S(1)} custom-call(f32[4,128,128]{2,1,0:T(8,128)S(1)} %convolution_subtract_fusion.6), custom_call_target="Cholesky" | custom-call | tf_op jit(solution)/shard_map/while/body/eval_jaxpr/jit(cholesky)/cholesky | solution.py:83
  462.8 3.9 while.18
  463.5 1.3 bitcast_dynamic-update-slice_fusion.5
  465.4 1.3 bitcast_dynamic-update-slice_fusion.5
  466.7 78.6 %custom-call.48 = f32[4,2,128,128]{2,3,1,0:T(8,128)S(1)} custom-call(f32[4,2,128,128]{3,2,1,0:T(8,128)S(1)} %bitcast.583), custom_call_target="InvertDiagBlocksLowerTriangular" | custom-call | tf_op jit(solution)/shard_map/while/body/eval_jaxpr/jit(_cho_solve)/vmap()/triangular_solve | solution.py:86
  547.0 0.6 fusion.72
  548.2 0.6 convolution_subtract_fusion.8
  549.7 1.0 copy-done
  550.7 1.0 copy-done.1
  (196 shorter events, 29.2 us)
Async XLA Ops:
  0.1 8.9 %copy-start.2 = (s32[16]{0:T(128)S(1)}, s32[16]{0:T(128)}, u32[]{:S(2)}) copy-start(s32[16]{0:T(128)} %param.7) | copy-start | bytes 196
  43.8 21.4 %copy-start.3 = (s32[1,16]{1,0:T(1,128)S(1)}, s32[1,16]{1,0:T(1,128)}, u32[]{:S(2)}) copy-start(s32[1,16]{1,0:T(1,128)} %param.6) | copy-start | bytes 196
  45.6 33.2 %all-to-all-start = ((bf16[64,2,512]{2,1,0:T(2,128)(2,1)}), bf16[64,2,512]{2,1,0:T(2,128)(2,1)S(1)}, u32[]{:S(2)}, u32[]{:S(2)}) async-start(bf16[64,2,512]{2,1,0:T(2,128)(2,1)} %reshape.169), calls=%async_computation | async-start | bytes 262144 | tf_op jit(solution)/shard_map/all_to_all | solution.py:16
  323.2 1.2 copy-start
  324.4 1.0 copy-start.1
  549.4 1.2 copy-start
  550.7 1.0 copy-start.1
